TPU v7x, 512 devices: a whole 4x4x16 slice. The times are simulated.
512 devices in a mesh: gx: 8 (over y, core), gy: 4 (over x), gz: 16 (over z).
Axes of the slice: x: 4, y: 4, z: 16, core: 2. Of those that a mesh axis runs over, the one named last changes fastest.
Arguments:
- level_set: float32 [128, 64, 2048], P('gx', 'gy', 'gz'), may hold values from 0 to 1
- velocity: float32 [3, 128, 64, 2048], P(None, 'gx', 'gy', 'gz'), may hold values from -6 to 6
- source: float32 [128, 64, 2048], P('gx', 'gy', 'gz'), may hold values from -6 to 6
- coarse_factor: float32 [512, 512], P(('gx', 'gy', 'gz')), may hold values from -0.2 to 0.2
Outputs:
- level_set_new: float32 [128, 64, 2048], P('gx', 'gy', 'gz')
- pressure: float32 [128, 64, 2048], P('gx', 'gy', 'gz')
All inputs are finite; a program needn't handle non-finite values.
Results may differ from a plain program's by a relative error of at most 0.029.
Values sent between devices are 32-bit elements; how exact they have to be, the bound alone decides.
A program may use at most 64 MiB of HBM per device.

v0:
```python
import jax
import jax.numpy as jnp
import numpy as np
from jax import lax
from jax.sharding import PartitionSpec as P

NP = 8
RSWEEPS = 2
ITERS = 6
GLL_POINTS = (
    -1.0,
    -0.8717401485096066,
    -0.5917001814331423,
    -0.2092992179024789,
    0.2092992179024789,
    0.5917001814331423,
    0.8717401485096066,
    1.0,
)
GLL_WEIGHTS = (
    0.03571428571428571,
    0.21070422714350603,
    0.3411226924835044,
    0.4124587946587038,
    0.4124587946587038,
    0.3411226924835044,
    0.21070422714350603,
    0.03571428571428571,
)
HIGHEST = lax.Precision.HIGHEST
TIME_STEP = 0.02
PSEUDO_STEP = 0.004
INTERFACE_WIDTH = 0.5
GAS_DENSITY = 0.1
SOURCE_SCALE = 20.0


def extended(cells, sides, width):
    for axis, dim in sides:
        count = lax.axis_size(axis)
        ends = count - 1
        head = lax.slice_in_dim(cells, 0, width, axis=dim)
        tail = lax.slice_in_dim(cells, cells.shape[dim] - width, cells.shape[dim], axis=dim)
        cells = jnp.concatenate(
            [
                lax.ppermute(tail, axis, [(i, (i + 1) % count) for i in range(ends)]),
                cells,
                lax.ppermute(head, axis, [((i + 1) % count, i) for i in range(ends)]),
            ],
            axis=dim,
        )
    return cells


def node_tables():
    points = np.array(GLL_POINTS)
    amount = points.shape[0]
    barycentric = np.ones(amount)
    for target in range(amount):
        for partner in range(amount):
            if partner != target:
                barycentric[target] = barycentric[target] / (points[target] - points[partner])
    derivative = np.zeros((amount, amount))
    for target in range(amount):
        for partner in range(amount):
            if partner != target:
                derivative[target, partner] = (
                    barycentric[partner] / barycentric[target] / (points[target] - points[partner])
                )
        derivative[target, target] = -np.sum(derivative[target])
    return derivative


def apply_axis(values, matrix, which_axis):
    if which_axis == 0:
        return jnp.einsum("ap,pqr->aqr", matrix, values, precision=HIGHEST)
    if which_axis == 1:
        return jnp.einsum("aq,pqr->par", matrix, values, precision=HIGHEST)
    return jnp.einsum("pqr,ar->pqa", values, matrix, precision=HIGHEST)


def edge_passes(padded):
    summed = padded
    for which_axis in (1, 2, 3):
        amount = summed.shape[which_axis] - 2
        center = lax.slice_in_dim(summed, 1, amount + 1, axis=which_axis)
        upper_side = lax.slice_in_dim(summed, 2, amount + 2, axis=which_axis)
        lower_side = lax.slice_in_dim(summed, 0, amount, axis=which_axis)
        shape_list = [1, 1, 1, 1]
        shape_list[which_axis] = amount
        position = (jnp.arange(amount) % NP).reshape(shape_list)
        summed = (
            center
            + jnp.where(position == NP - 1, upper_side, 0.0)
            + jnp.where(position == 0, lower_side, 0.0)
        )
    return summed


def assemble(stacked):
    padded = extended(stacked, (("gx", 1), ("gy", 2), ("gz", 3)), 1)
    return edge_passes(padded)


def body(level_set, velocity, source, coarse_factor):
    shape_tuple = level_set.shape
    derivative = node_tables()
    deriv_tables = [
        jnp.asarray(np.kron(np.eye(extent // NP), derivative), jnp.float32)
        for extent in shape_tuple
    ]
    trans_tables = [
        jnp.asarray(np.kron(np.eye(extent // NP), derivative.T), jnp.float32)
        for extent in shape_tuple
    ]
    square_tables = [
        jnp.asarray(np.kron(np.eye(extent // NP), (derivative * derivative).T), jnp.float32)
        for extent in shape_tuple
    ]
    weights = jnp.asarray(np.array(GLL_WEIGHTS), jnp.float32)
    along_x = jnp.tile(weights, shape_tuple[0] // NP)
    along_y = jnp.tile(weights, shape_tuple[1] // NP)
    along_z = jnp.tile(weights, shape_tuple[2] // NP)
    bmass = along_x[:, None, None] * along_y[None, :, None] * along_z[None, None, :]
    gradient = [
        apply_axis(level_set, deriv_tables[which_axis], which_axis) for which_axis in range(3)
    ]
    advect = velocity[0] * gradient[0] + velocity[1] * gradient[1] + velocity[2] * gradient[2]
    divergence = (
        apply_axis(bmass * velocity[0], trans_tables[0], 0)
        + apply_axis(bmass * velocity[1], trans_tables[1], 1)
        + apply_axis(bmass * velocity[2], trans_tables[2], 2)
        + bmass * source
    )
    assembled = assemble(jnp.stack([bmass * advect, bmass, divergence]))
    mass_sum = assembled[1]
    weight = bmass / mass_sum
    level_now = level_set - TIME_STEP * assembled[0] / mass_sum
    rhs_field = SOURCE_SCALE * assembled[2]
    for sweep in range(RSWEEPS):
        gradient = [
            apply_axis(level_now, deriv_tables[which_axis], which_axis) for which_axis in range(3)
        ]
        inv_norm = 1.0 / jnp.sqrt(
            1.0 + gradient[0] * gradient[0] + gradient[1] * gradient[1] + gradient[2] * gradient[2]
        )
        compress = level_now * (1.0 - level_now) * inv_norm
        weak_form = apply_axis(
            bmass * (compress * gradient[0] - INTERFACE_WIDTH * gradient[0]), trans_tables[0], 0
        )
        weak_form = weak_form + apply_axis(
            bmass * (compress * gradient[1] - INTERFACE_WIDTH * gradient[1]), trans_tables[1], 1
        )
        weak_form = weak_form + apply_axis(
            bmass * (compress * gradient[2] - INTERFACE_WIDTH * gradient[2]), trans_tables[2], 2
        )
        level_now = level_now + PSEUDO_STEP * assemble(weak_form[None])[0] / mass_sum
    inverse_density = 1.0 / (GAS_DENSITY + (1.0 - GAS_DENSITY) * jnp.clip(level_now, 0.0, 1.0))
    scaled = bmass * inverse_density
    diag_local = (
        apply_axis(scaled, square_tables[0], 0)
        + apply_axis(scaled, square_tables[1], 1)
        + apply_axis(scaled, square_tables[2], 2)
        + bmass
    )
    diagonal = assemble(diag_local[None])[0]
    own_row = coarse_factor[0]

    def precondition(residual):
        jacobi = residual / diagonal
        restricted = jnp.sum(weight * residual)
        coarse_mid = lax.psum(restricted * own_row, ("gx", "gy", "gz"))
        coarse_value = jnp.dot(own_row, coarse_mid, precision=HIGHEST)
        result = jacobi + assemble((weight * coarse_value)[None])[0]
        return (result, lax.psum(jnp.sum(weight * residual * result), ("gx", "gy", "gz")))

    pressure = jnp.zeros_like(rhs_field)
    residual = rhs_field
    direction, inner_now = precondition(residual)
    for step in range(ITERS):
        local_part = bmass * direction
        for element_which_axis in range(3):
            local_part = local_part + apply_axis(
                scaled
                * apply_axis(direction, deriv_tables[element_which_axis], element_which_axis),
                trans_tables[element_which_axis],
                element_which_axis,
            )
        image = assemble(local_part[None])[0]
        curvature = lax.psum(jnp.sum(weight * direction * image), ("gx", "gy", "gz"))
        step_size = inner_now / curvature
        pressure = pressure + step_size * direction
        residual = residual - step_size * image
        if step + 1 < ITERS:
            preconditioned, inner_next = precondition(residual)
            direction = preconditioned + inner_next / inner_now * direction
            inner_now = inner_next
    return (level_now, pressure)


def solution(mesh):
    in_specs = (
        P("gx", "gy", "gz"),
        P(None, "gx", "gy", "gz"),
        P("gx", "gy", "gz"),
        P(("gx", "gy", "gz"), None),
    )
    out_specs = (P("gx", "gy", "gz"), P("gx", "gy", "gz"))
    return jax.shard_map(body, mesh=mesh, in_specs=in_specs, out_specs=out_specs, check_vma=False)
```

profile of v0, /device:TPU:1, one launch (start us, length us, event | category | flops | bytes accessed | tf_op | source)
XLA Modules:
  0.0 2206.5 jit_solution(12459862347474892173)
XLA Ops:
  6.2 4.6 collective-permute-start
  10.8 5.5 collective-permute-start.1
  20.4 3.9 collective-permute-done.3
  30.4 3.4 collective-permute-done.5
  37.9 4.1 collective-permute-start.6
  54.7 3.6 collective-permute-start.10
  59.6 3.9 collective-permute-done.10
  63.5 5.4 collective-permute-done.11
  71.4 3.7 collective-permute-start.12
  87.6 4.9 collective-permute-start.16
  93.8 3.9 collective-permute-done.16
  97.7 3.8 collective-permute-done.17
  103.5 104.3 %psum.126 = f32[512]{0:T(512)S(1)} all-reduce(f32[512]{0:T(512)S(1)} %broadcast_multiply_fusion.13), channel_id=1, replica_groups=mesh['gx'=8,'gy'=4,'gz'=16] {'gx','gy','gz'}, use_global_device_ids=true, to_apply=%region_1.2 | all-reduce | flops 512 | bytes 4096 | tf_op jit(solution)/shard_map/psum | solution.py:172
  223.2 4.0 collective-permute-start.20
  231.8 3.9 collective-permute-start.22
  240.6 4.4 collective-permute-done.23
  247.7 3.5 collective-permute-start.30
  256.2 4.3 collective-permute-start.32
  269.5 3.9 collective-permute-done.34
  273.4 4.8 collective-permute-done.35
  279.6 104.5 %all-reduce = (f32[]{:T(128)}, f32[]{:T(128)}) all-reduce(f32[]{:T(128)} %get-tuple-element.9, f32[]{:T(128)} %get-tuple-element.8), channel_id=1, replica_groups=mesh['gx'=8,'gy'=4,'gz'=16] {'gx','gy','gz'}, use_global_device_ids=true, to_apply=%region_3.4 | all-reduce | flops 2 | bytes 16 | tf_op jit(solution)/shard_map/psum | solution.py:175
  386.8 98.4 %psum.129 = f32[512]{0:T(512)S(1)} all-reduce(f32[512]{0:T(512)S(1)} %broadcast_multiply_fusion.12), channel_id=1, replica_groups=mesh['gx'=8,'gy'=4,'gz'=16] {'gx','gy','gz'}, use_global_device_ids=true, to_apply=%region_7.8 | all-reduce | flops 512 | bytes 4096 | tf_op jit(solution)/shard_map/psum | solution.py:172
  497.0 3.4 collective-permute-done.39
  500.5 3.7 collective-permute-start.40
  505.5 3.7 collective-permute-done.40
  509.2 3.9 collective-permute-done.41
  514.5 101.3 %psum.130 = f32[]{:T(128)} all-reduce(f32[]{:T(128)} %get-tuple-element.36), channel_id=1, replica_groups=mesh['gx'=8,'gy'=4,'gz'=16] {'gx','gy','gz'}, use_global_device_ids=true, to_apply=%region_9.10 | all-reduce | flops 1 | bytes 8 | tf_op jit(solution)/shard_map/psum | solution.py:175
  636.6 3.9 collective-permute-done.46
  640.5 3.8 collective-permute-done.47
  645.7 102.2 %psum.131 = f32[]{:T(128)} all-reduce(f32[]{:T(128)} %get-tuple-element.34), channel_id=1, replica_groups=mesh['gx'=8,'gy'=4,'gz'=16] {'gx','gy','gz'}, use_global_device_ids=true, to_apply=%region_11.12 | all-reduce | flops 1 | bytes 8 | tf_op jit(solution)/shard_map/psum | solution.py:190
  750.5 99.1 %psum.132 = f32[512]{0:T(512)S(1)} all-reduce(f32[512]{0:T(512)S(1)} %broadcast_multiply_fusion.11), channel_id=1, replica_groups=mesh['gx'=8,'gy'=4,'gz'=16] {'gx','gy','gz'}, use_global_device_ids=true, to_apply=%region_13.14 | all-reduce | flops 512 | bytes 4096 | tf_op jit(solution)/shard_map/psum | solution.py:172
  861.8 3.4 collective-permute-done.51
  865.3 3.7 collective-permute-start.52
  870.3 3.7 collective-permute-done.52
  874.0 3.9 collective-permute-done.53
  879.3 100.7 %psum.133 = f32[]{:T(128)} all-reduce(f32[]{:T(128)} %get-tuple-element.30), channel_id=1, replica_groups=mesh['gx'=8,'gy'=4,'gz'=16] {'gx','gy','gz'}, use_global_device_ids=true, to_apply=%region_15.16 | all-reduce | flops 1 | bytes 8 | tf_op jit(solution)/shard_map/psum | solution.py:175
  1000.7 3.9 collective-permute-done.58
  1004.6 3.8 collective-permute-done.59
  1009.8 102.3 %psum.134 = f32[]{:T(128)} all-reduce(f32[]{:T(128)} %get-tuple-element.28), channel_id=1, replica_groups=mesh['gx'=8,'gy'=4,'gz'=16] {'gx','gy','gz'}, use_global_device_ids=true, to_apply=%region_17.18 | all-reduce | flops 1 | bytes 8 | tf_op jit(solution)/shard_map/psum | solution.py:190
  1114.7 98.7 %psum.135 = f32[512]{0:T(512)S(1)} all-reduce(f32[512]{0:T(512)S(1)} %broadcast_multiply_fusion.10), channel_id=1, replica_groups=mesh['gx'=8,'gy'=4,'gz'=16] {'gx','gy','gz'}, use_global_device_ids=true, to_apply=%region_19.20 | all-reduce | flops 512 | bytes 4096 | tf_op jit(solution)/shard_map/psum | solution.py:172
  1225.6 3.4 collective-permute-done.63
  1229.1 3.7 collective-permute-start.64
  1234.1 3.7 collective-permute-done.64
  1237.8 3.9 collective-permute-done.65
  1243.1 100.7 %psum.136 = f32[]{:T(128)} all-reduce(f32[]{:T(128)} %get-tuple-element.24), channel_id=1, replica_groups=mesh['gx'=8,'gy'=4,'gz'=16] {'gx','gy','gz'}, use_global_device_ids=true, to_apply=%region_21.22 | all-reduce | flops 1 | bytes 8 | tf_op jit(solution)/shard_map/psum | solution.py:175
  1364.5 3.9 collective-permute-done.70
  1368.4 3.8 collective-permute-done.71
  1373.6 102.5 %psum.137 = f32[]{:T(128)} all-reduce(f32[]{:T(128)} %get-tuple-element.22), channel_id=1, replica_groups=mesh['gx'=8,'gy'=4,'gz'=16] {'gx','gy','gz'}, use_global_device_ids=true, to_apply=%region_23.24 | all-reduce | flops 1 | bytes 8 | tf_op jit(solution)/shard_map/psum | solution.py:190
  1478.7 98.7 %psum.138 = f32[512]{0:T(512)S(1)} all-reduce(f32[512]{0:T(512)S(1)} %broadcast_multiply_fusion.9), channel_id=1, replica_groups=mesh['gx'=8,'gy'=4,'gz'=16] {'gx','gy','gz'}, use_global_device_ids=true, to_apply=%region_25.26 | all-reduce | flops 512 | bytes 4096 | tf_op jit(solution)/shard_map/psum | solution.py:172
  1593.1 3.7 collective-permute-start.76
  1598.1 3.7 collective-permute-done.76
  1601.8 3.9 collective-permute-done.77
  1607.0 100.7 %psum.139 = f32[]{:T(128)} all-reduce(f32[]{:T(128)} %get-tuple-element.18), channel_id=1, replica_groups=mesh['gx'=8,'gy'=4,'gz'=16] {'gx','gy','gz'}, use_global_device_ids=true, to_apply=%region_27.28 | all-reduce | flops 1 | bytes 8 | tf_op jit(solution)/shard_map/psum | solution.py:175
  1728.4 3.9 collective-permute-done.82
  1732.3 3.8 collective-permute-done.83
  1737.5 102.3 %psum.140 = f32[]{:T(128)} all-reduce(f32[]{:T(128)} %get-tuple-element.16), channel_id=1, replica_groups=mesh['gx'=8,'gy'=4,'gz'=16] {'gx','gy','gz'}, use_global_device_ids=true, to_apply=%region_29.30 | all-reduce | flops 1 | bytes 8 | tf_op jit(solution)/shard_map/psum | solution.py:190
  1842.5 98.7 %psum.141 = f32[512]{0:T(512)S(1)} all-reduce(f32[512]{0:T(512)S(1)} %broadcast_multiply_fusion.8), channel_id=1, replica_groups=mesh['gx'=8,'gy'=4,'gz'=16] {'gx','gy','gz'}, use_global_device_ids=true, to_apply=%region_31.32 | all-reduce | flops 512 | bytes 4096 | tf_op jit(solution)/shard_map/psum | solution.py:172
  1956.9 3.7 collective-permute-start.88
  1961.9 3.7 collective-permute-done.88
  1965.6 3.9 collective-permute-done.89
  1970.8 100.7 %psum.142 = f32[]{:T(128)} all-reduce(f32[]{:T(128)} %get-tuple-element.12), channel_id=1, replica_groups=mesh['gx'=8,'gy'=4,'gz'=16] {'gx','gy','gz'}, use_global_device_ids=true, to_apply=%region_33.34 | all-reduce | flops 1 | bytes 8 | tf_op jit(solution)/shard_map/psum | solution.py:175
  2092.3 3.9 collective-permute-done.94
  2096.2 3.8 collective-permute-done.95
  2102.2 102.1 %psum.143 = f32[]{:T(128)} all-reduce(f32[]{:T(128)} %fusion.92), channel_id=1, replica_groups=mesh['gx'=8,'gy'=4,'gz'=16] {'gx','gy','gz'}, use_global_device_ids=true, to_apply=%region_35.36 | all-reduce | flops 1 | bytes 8 | tf_op jit(solution)/shard_map/psum | solution.py:190
  (397 shorter events, 285.7 us)
Async XLA Ops:
  6.2 10.1 collective-permute-start
  10.8 6.3 collective-permute-start.1
  19.1 5.2 collective-permute-start.3
  25.1 4.8 collective-permute-start.4
  28.6 5.2 collective-permute-start.5
  37.9 6.1 collective-permute-start.6
  42.0 5.0 collective-permute-start.7
  54.7 8.8 collective-permute-start.10
  58.3 10.6 collective-permute-start.11
  71.4 5.7 collective-permute-start.12
  75.2 5.0 collective-permute-start.13
  87.6 10.1 collective-permute-start.16
  92.5 9.1 collective-permute-start.17
  209.1 10.4 collective-permute-start.24
  211.1 8.4 collective-permute-start.25
  214.4 8.8 collective-permute-start.18
  217.6 5.6 collective-permute-start.19
  219.6 9.2 collective-permute-start.26
  221.9 6.8 collective-permute-start.27
  223.2 8.3 collective-permute-start.20
  228.9 8.1 collective-permute-start.28
  230.2 8.5 collective-permute-start.29
  231.8 8.8 collective-permute-start.22
  235.7 9.3 collective-permute-start.23
  247.7 5.5 collective-permute-start.30
  251.3 5.0 collective-permute-start.31
  256.2 5.6 collective-permute-start.32
  265.1 8.3 collective-permute-start.34
  268.2 10.0 collective-permute-start.35
  489.3 5.0 collective-permute-start.37
  495.7 4.7 collective-permute-start.39
  500.5 8.7 collective-permute-start.40
  504.2 8.9 collective-permute-start.41
  621.0 5.0 collective-permute-start.43
  632.6 7.9 collective-permute-start.46
  635.3 9.1 collective-permute-start.47
  851.0 5.0 collective-permute-start.48
  854.0 5.0 collective-permute-start.49
  865.3 8.7 collective-permute-start.52
  869.0 8.9 collective-permute-start.53
  985.3 5.0 collective-permute-start.55
  996.9 7.7 collective-permute-start.58
  999.4 9.1 collective-permute-start.59
  1214.8 5.0 collective-permute-start.60
  1217.8 5.0 collective-permute-start.61
  1229.1 8.7 collective-permute-start.64
  1232.8 8.9 collective-permute-start.65
  1349.1 5.0 collective-permute-start.67
  1360.7 7.7 collective-permute-start.70
  1363.2 9.1 collective-permute-start.71
  1578.8 5.0 collective-permute-start.72
  1581.8 5.0 collective-permute-start.73
  1593.1 8.7 collective-permute-start.76
  1596.8 8.9 collective-permute-start.77
  1713.1 5.0 collective-permute-start.79
  1724.7 7.7 collective-permute-start.82
  1727.1 9.1 collective-permute-start.83
  1942.5 5.0 collective-permute-start.84
  1945.6 5.0 collective-permute-start.85
  1956.9 8.7 collective-permute-start.88
  1960.6 8.9 collective-permute-start.89
  2076.8 5.0 collective-permute-start.91
  2088.5 7.8 collective-permute-start.94
  2091.0 9.1 collective-permute-start.95
  (41 other events, 373.7 us)
where the time goes:
time: 2220 us; the launch traced here: 2210 us
  blocking collectives  1720 us (77%)
  starting transfers between devices  211 us (10%)
  waiting for transfers between devices  199 us (9%)
  other arithmetic  36.4 us (2%)
    psum x6, blocking collectives, precondition(): lax.psum(jnp.sum(weight * residual * result), ('gx', 'gy', 'gz'))  609 us
    psum x6, blocking collectives, precondition(): coarse_mid = lax.psum(restricted * own_row, ('gx', 'gy', 'gz'))  598 us
    psum x5, blocking collectives, body(): lax.psum(jnp.sum(weight * direction * image), ('gx', 'gy', 'gz'))  511 us
    ppermute x48, waiting for transfers between devices, extended(): lax.ppermute(head, axis, [((i + 1) % count, i) for i in range(ends)])  147 us
    ppermute x48, starting transfers between devices, extended(): lax.ppermute(tail, axis, [(i, (i + 1) % count) for i in range(ends)])  133 us
    ppermute x48, starting transfers between devices, extended(): lax.ppermute(head, axis, [((i + 1) % count, i) for i in range(ends)])  77.4 us
    ppermute x48, waiting for transfers between devices, extended(): lax.ppermute(tail, axis, [(i, (i + 1) % count) for i in range(ends)])  51.5 us
  transfers between devices with their start and end apart: 96, of which 59 were waited for; matrix products, arithmetic and copies ran while one was open for 0% of the time, Pallas kernels for 0%

commit v1 on v0

--- a/solution.py
+++ b/solution.py
@@ -169,7 +169,7 @@
     def precondition(residual):
         jacobi = residual / diagonal
         restricted = jnp.sum(weight * residual)
-        coarse_mid = lax.psum(restricted * own_row, ("gx", "gy", "gz"))
+        coarse_mid = jnp.sum(lax.all_gather(restricted * own_row, ("gx", "gy", "gz")), axis=0)
         coarse_value = jnp.dot(own_row, coarse_mid, precision=HIGHEST)
         result = jacobi + assemble((weight * coarse_value)[None])[0]
         return (result, lax.psum(jnp.sum(weight * residual * result), ("gx", "gy", "gz")))

time: 2220 us -> 2620 us (1.18)
  waiting for transfers between devices: 199 us -> 1160 us
  blocking collectives: 1720 us -> 1120 us
    all_gather x0 -> x6, waiting for transfers between devices: none -> 959 us  [precondition(): lax.all_gather(restricted * own_row, ('gx', 'gy', 'gz'))]
    psum x6 -> x0, blocking collectives: 598 us -> none  [precondition(): coarse_mid = lax.psum(restricted * own_row, ('gx', 'gy', 'gz'))]
  transfers between devices with their start and end apart: 96 -> 102, of which waited for: 59 -> 66; matrix products, arithmetic and copies ran while one was open for 0% -> 0% of each run, Pallas kernels for 0% -> 0%
where the time goes in v1:
time: 2620 us; the launch traced here: 2610 us
  waiting for transfers between devices  1160 us (44%)
  blocking collectives  1120 us (43%)
  starting transfers between devices  221 us (8%)
  other arithmetic  50.9 us (2%)
  between operations  31.5 us (1%)
    all_gather x6, waiting for transfers between devices, precondition(): lax.all_gather(restricted * own_row, ('gx', 'gy', 'gz'))  959 us
    psum x6, blocking collectives, precondition(): lax.psum(jnp.sum(weight * residual * result), ('gx', 'gy', 'gz'))  607 us
    psum x5, blocking collectives, body(): lax.psum(jnp.sum(weight * direction * image), ('gx', 'gy', 'gz'))  511 us
    ppermute x48, waiting for transfers between devices, extended(): lax.ppermute(head, axis, [((i + 1) % count, i) for i in range(ends)])  149 us
    ppermute x48, starting transfers between devices, extended(): lax.ppermute(tail, axis, [(i, (i + 1) % count) for i in range(ends)])  142 us
    ppermute x48, starting transfers between devices, extended(): lax.ppermute(head, axis, [((i + 1) % count, i) for i in range(ends)])  78 us
    ppermute x48, waiting for transfers between devices, extended(): lax.ppermute(tail, axis, [(i, (i + 1) % count) for i in range(ends)])  52.6 us
  transfers between devices with their start and end apart: 102, of which 66 were waited for; matrix products, arithmetic and copies ran while one was open for 0% of the time, Pallas kernels for 0%

profile of v1, /device:TPU:1, one launch (start us, length us, event | category | flops | bytes accessed | tf_op | source)
XLA Modules:
  0.0 2606.5 jit_solution(18407238822878960591)
XLA Ops:
  12.8 4.6 collective-permute-start
  17.4 5.5 collective-permute-start.1
  27.0 3.9 collective-permute-done.3
  37.0 3.4 collective-permute-done.5
  44.4 4.1 collective-permute-start.6
  61.3 3.6 collective-permute-start.10
  66.1 3.9 collective-permute-done.10
  70.1 5.4 collective-permute-done.11
  78.0 3.7 collective-permute-start.12
  94.2 4.9 collective-permute-start.16
  100.3 3.9 collective-permute-done.16
  104.2 3.8 collective-permute-done.17
  111.6 3.2 collective-permute-start.18
  123.6 151.8 %all-gather.13.cloned.1.call-done = f32[512,1,512]{2,1,0:T(1,128)} async-done(((f32[1,1,512]{2,1,0:T(1,128)}), f32[512,1,512]{2,1,0:T(1,128)}) %all-gather.13.cloned.1.call-update) | async-done | bytes 1048592 | tf_op jit(solution)/shard_map/all_gather | solution.py:172
  278.6 3.3 collective-permute-start.24
  295.9 4.0 collective-permute-start.28
  304.5 4.1 collective-permute-done.29
  311.3 4.0 collective-permute-start.30
  320.3 4.0 collective-permute-start.32
  332.6 3.9 collective-permute-done.34
  336.5 3.8 collective-permute-done.35
  341.7 102.6 %all-reduce = (f32[]{:T(128)}, f32[]{:T(128)}) all-reduce(f32[]{:T(128)} %get-tuple-element.9, f32[]{:T(128)} %get-tuple-element.8), channel_id=1, replica_groups=mesh['gx'=8,'gy'=4,'gz'=16] {'gx','gy','gz'}, use_global_device_ids=true, to_apply=%region_3.4 | all-reduce | flops 2 | bytes 16 | tf_op jit(solution)/shard_map/psum | solution.py:175
  447.7 161.5 %all-gather.15.cloned.1.call-done = f32[512,1,512]{2,1,0:T(1,128)} async-done(((f32[1,1,512]{2,1,0:T(1,128)}), f32[512,1,512]{2,1,0:T(1,128)}) %all-gather.15.cloned.1.call-update) | async-done | bytes 1048592 | tf_op jit(solution)/shard_map/all_gather | solution.py:172
  612.3 3.3 collective-permute-start.36
  625.0 3.1 collective-permute-done.39
  632.4 3.9 collective-permute-done.40
  636.4 3.8 collective-permute-done.41
  641.5 100.8 %psum.86 = f32[]{:T(128)} all-reduce(f32[]{:T(128)} %get-tuple-element.36), channel_id=1, replica_groups=mesh['gx'=8,'gy'=4,'gz'=16] {'gx','gy','gz'}, use_global_device_ids=true, to_apply=%region_9.10 | all-reduce | flops 1 | bytes 8 | tf_op jit(solution)/shard_map/psum | solution.py:175
  763.3 3.9 collective-permute-done.46
  767.2 3.8 collective-permute-done.47
  772.4 102.2 %psum.87 = f32[]{:T(128)} all-reduce(f32[]{:T(128)} %get-tuple-element.34), channel_id=1, replica_groups=mesh['gx'=8,'gy'=4,'gz'=16] {'gx','gy','gz'}, use_global_device_ids=true, to_apply=%region_11.12 | all-reduce | flops 1 | bytes 8 | tf_op jit(solution)/shard_map/psum | solution.py:190
  877.9 161.6 %all-gather.17.cloned.1.call-done = f32[512,1,512]{2,1,0:T(1,128)} async-done(((f32[1,1,512]{2,1,0:T(1,128)}), f32[512,1,512]{2,1,0:T(1,128)}) %all-gather.17.cloned.1.call-update) | async-done | bytes 1048592 | tf_op jit(solution)/shard_map/all_gather | solution.py:172
  1042.7 3.3 collective-permute-start.48
  1051.0 3.3 collective-permute-start.50
  1063.0 3.9 collective-permute-done.52
  1067.0 3.8 collective-permute-done.53
  1072.2 100.8 %psum.88 = f32[]{:T(128)} all-reduce(f32[]{:T(128)} %get-tuple-element.30), channel_id=1, replica_groups=mesh['gx'=8,'gy'=4,'gz'=16] {'gx','gy','gz'}, use_global_device_ids=true, to_apply=%region_15.16 | all-reduce | flops 1 | bytes 8 | tf_op jit(solution)/shard_map/psum | solution.py:175
  1193.9 3.9 collective-permute-done.58
  1197.8 3.8 collective-permute-done.59
  1203.0 102.2 %psum.89 = f32[]{:T(128)} all-reduce(f32[]{:T(128)} %get-tuple-element.28), channel_id=1, replica_groups=mesh['gx'=8,'gy'=4,'gz'=16] {'gx','gy','gz'}, use_global_device_ids=true, to_apply=%region_17.18 | all-reduce | flops 1 | bytes 8 | tf_op jit(solution)/shard_map/psum | solution.py:190
  1308.5 161.6 %all-gather.19.cloned.1.call-done = f32[512,1,512]{2,1,0:T(1,128)} async-done(((f32[1,1,512]{2,1,0:T(1,128)}), f32[512,1,512]{2,1,0:T(1,128)}) %all-gather.19.cloned.1.call-update) | async-done | bytes 1048592 | tf_op jit(solution)/shard_map/all_gather | solution.py:172
  1473.4 3.3 collective-permute-start.60
  1493.4 3.9 collective-permute-done.64
  1497.4 3.8 collective-permute-done.65
  1502.5 100.8 %psum.90 = f32[]{:T(128)} all-reduce(f32[]{:T(128)} %get-tuple-element.24), channel_id=1, replica_groups=mesh['gx'=8,'gy'=4,'gz'=16] {'gx','gy','gz'}, use_global_device_ids=true, to_apply=%region_21.22 | all-reduce | flops 1 | bytes 8 | tf_op jit(solution)/shard_map/psum | solution.py:175
  1624.3 3.9 collective-permute-done.70
  1628.2 3.8 collective-permute-done.71
  1633.4 102.2 %psum.91 = f32[]{:T(128)} all-reduce(f32[]{:T(128)} %get-tuple-element.22), channel_id=1, replica_groups=mesh['gx'=8,'gy'=4,'gz'=16] {'gx','gy','gz'}, use_global_device_ids=true, to_apply=%region_23.24 | all-reduce | flops 1 | bytes 8 | tf_op jit(solution)/shard_map/psum | solution.py:190
  1739.2 161.3 %all-gather.21.cloned.1.call-done = f32[512,1,512]{2,1,0:T(1,128)} async-done(((f32[1,1,512]{2,1,0:T(1,128)}), f32[512,1,512]{2,1,0:T(1,128)}) %all-gather.21.cloned.1.call-update) | async-done | bytes 1048592 | tf_op jit(solution)/shard_map/all_gather | solution.py:172
  1903.7 3.3 collective-permute-start.72
  1923.8 3.9 collective-permute-done.76
  1927.7 3.8 collective-permute-done.77
  1932.9 100.8 %psum.92 = f32[]{:T(128)} all-reduce(f32[]{:T(128)} %get-tuple-element.18), channel_id=1, replica_groups=mesh['gx'=8,'gy'=4,'gz'=16] {'gx','gy','gz'}, use_global_device_ids=true, to_apply=%region_27.28 | all-reduce | flops 1 | bytes 8 | tf_op jit(solution)/shard_map/psum | solution.py:175
  2054.7 3.9 collective-permute-done.82
  2058.6 3.8 collective-permute-done.83
  2063.8 102.2 %psum.93 = f32[]{:T(128)} all-reduce(f32[]{:T(128)} %get-tuple-element.16), channel_id=1, replica_groups=mesh['gx'=8,'gy'=4,'gz'=16] {'gx','gy','gz'}, use_global_device_ids=true, to_apply=%region_29.30 | all-reduce | flops 1 | bytes 8 | tf_op jit(solution)/shard_map/psum | solution.py:190
  2169.3 161.6 %all-gather.23.cloned.1.call-done = f32[512,1,512]{2,1,0:T(1,128)} async-done(((f32[1,1,512]{2,1,0:T(1,128)}), f32[512,1,512]{2,1,0:T(1,128)}) %all-gather.23.cloned.1.call-update) | async-done | bytes 1048592 | tf_op jit(solution)/shard_map/all_gather | solution.py:172
  2334.2 3.3 collective-permute-start.84
  2354.2 3.9 collective-permute-done.88
  2358.2 3.8 collective-permute-done.89
  2363.3 100.8 %psum.94 = f32[]{:T(128)} all-reduce(f32[]{:T(128)} %get-tuple-element.12), channel_id=1, replica_groups=mesh['gx'=8,'gy'=4,'gz'=16] {'gx','gy','gz'}, use_global_device_ids=true, to_apply=%region_33.34 | all-reduce | flops 1 | bytes 8 | tf_op jit(solution)/shard_map/psum | solution.py:175
  2485.1 3.9 collective-permute-done.94
  2489.0 3.8 collective-permute-done.95
  2494.9 102.2 %psum.95 = f32[]{:T(128)} all-reduce(f32[]{:T(128)} %fusion.92), channel_id=1, replica_groups=mesh['gx'=8,'gy'=4,'gz'=16] {'gx','gy','gz'}, use_global_device_ids=true, to_apply=%region_35.36 | all-reduce | flops 1 | bytes 8 | tf_op jit(solution)/shard_map/psum | solution.py:190
  (415 shorter events, 316.4 us)
Async XLA Ops:
  7.2 268.2 %all-gather.13.cloned.1.call-start = ((), (), s32[]{:S(2)}) async-start(), calls=%async_computation | async-start | bytes 1050624 | tf_op jit(solution)/shard_map/all_gather | solution.py:172
  12.8 10.1 collective-permute-start
  17.4 6.3 collective-permute-start.1
  25.7 5.2 collective-permute-start.3
  35.1 5.2 collective-permute-start.5
  44.4 6.1 collective-permute-start.6
  48.6 5.0 collective-permute-start.7
  61.3 8.8 collective-permute-start.10
  64.8 10.6 collective-permute-start.11
  78.0 5.7 collective-permute-start.12
  81.8 5.0 collective-permute-start.13
  94.2 10.1 collective-permute-start.16
  99.0 9.1 collective-permute-start.17
  110.7 498.5 %all-gather.15.cloned.1.call-start = ((), (), s32[]{:S(2)}) async-start(), calls=%async_computation.1 | async-start | bytes 1050624 | tf_op jit(solution)/shard_map/all_gather | solution.py:172
  111.6 5.2 collective-permute-start.18
  114.8 5.0 collective-permute-start.19
  119.8 164.0 %collective-permute-start.20 = (f32[1,18,1,128]{3,1,2,0:T(8,128)S(1)}, f32[1,18,1,128]{3,1,2,0:T(8,128)S(1)}, u32[]{:S(2)}, u32[]{:S(2)}) collective-permute-start(f32[1,18,1,128]{3,1,2,0:T(8,128)S(1)} %get-tuple-element.111), channel_id=1, source_target_pairs={{0,16},{16,32},{32,48},{1,17},{17,33},{33,49},{2,18},{18,34},{34,5... | collective-permute-start | bytes 27656 | tf_op jit(solution)/shard_map/ppermute | solution.py:46
  122.3 161.6 %collective-permute-start.21 = (f32[1,18,1,128]{3,1,2,0:T(8,128)S(1)}, f32[1,18,1,128]{3,1,2,0:T(8,128)S(1)}, u32[]{:S(2)}, u32[]{:S(2)}) collective-permute-start(f32[1,18,1,128]{3,1,2,0:T(8,128)S(1)} %get-tuple-element.112), channel_id=1, source_target_pairs={{16,0},{32,16},{48,32},{17,1},{33,17},{49,33},{18,2},{34,18},{50,3... | collective-permute-start | bytes 27656 | tf_op jit(solution)/shard_map/ppermute | solution.py:48
  278.6 5.3 collective-permute-start.24
  281.9 5.0 collective-permute-start.25
  286.9 8.8 collective-permute-start.26
  290.0 5.7 collective-permute-start.27
  291.6 9.6 collective-permute-start.22
  294.4 8.2 collective-permute-start.23
  295.9 8.6 collective-permute-start.28
  299.9 8.7 collective-permute-start.29
  311.3 5.9 collective-permute-start.30
  315.3 5.0 collective-permute-start.31
  320.3 5.3 collective-permute-start.32
  328.9 7.6 collective-permute-start.34
  331.3 9.1 collective-permute-start.35
  447.6 591.9 %all-gather.17.cloned.1.call-start = ((), (), s32[]{:S(2)}) async-start(), calls=%async_computation.2 | async-start | bytes 1050624 | tf_op jit(solution)/shard_map/all_gather | solution.py:172
  612.3 5.2 collective-permute-start.36
  615.6 5.0 collective-permute-start.37
  628.3 8.0 collective-permute-start.40
  631.1 9.1 collective-permute-start.41
  747.4 5.0 collective-permute-start.43
  759.3 7.9 collective-permute-start.46
  762.0 9.1 collective-permute-start.47
  877.9 592.2 %all-gather.19.cloned.1.call-start = ((), (), s32[]{:S(2)}) async-start(), calls=%async_computation.3 | async-start | bytes 1050624 | tf_op jit(solution)/shard_map/all_gather | solution.py:172
  1042.7 5.2 collective-permute-start.48
  1046.0 5.0 collective-permute-start.49
  1058.9 8.0 collective-permute-start.52
  1061.7 9.1 collective-permute-start.53
  1178.0 5.0 collective-permute-start.55
  1189.9 7.9 collective-permute-start.58
  1192.6 9.1 collective-permute-start.59
  1308.5 592.0 %all-gather.21.cloned.1.call-start = ((), (), s32[]{:S(2)}) async-start(), calls=%async_computation.4 | async-start | bytes 1050624 | tf_op jit(solution)/shard_map/all_gather | solution.py:172
  1473.4 5.2 collective-permute-start.60
  1489.3 8.0 collective-permute-start.64
  1492.1 9.1 collective-permute-start.65
  1620.3 7.9 collective-permute-start.70
  1623.0 9.1 collective-permute-start.71
  1738.9 592.0 %all-gather.23.cloned.1.call-start = ((), (), s32[]{:S(2)}) async-start(), calls=%async_computation.5 | async-start | bytes 1050624 | tf_op jit(solution)/shard_map/all_gather | solution.py:172
  1903.7 5.2 collective-permute-start.72
  1919.7 8.0 collective-permute-start.76
  1922.5 9.1 collective-permute-start.77
  2050.7 7.9 collective-permute-start.82
  2053.4 9.1 collective-permute-start.83
  2334.2 5.2 collective-permute-start.84
  2350.1 8.0 collective-permute-start.88
  2352.9 9.1 collective-permute-start.89
  2481.1 7.9 collective-permute-start.94
  2483.8 9.1 collective-permute-start.95
  (47 other events, 194.2 us)
Sparse Core Ops, SparseCore 0:
  110.8 164.5 all-gather.12
  447.7 161.3 all-gather.14
  878.0 161.4 all-gather.16
  1308.6 161.4 all-gather.18
  1739.0 161.4 all-gather.20
  2169.4 161.4 all-gather.22
